TPU v7x, 32 devices: a whole 2x2x4 slice. The times are simulated.
32 devices in a mesh: tm: 4 (over y, x), space: 8 (over z, core).
Axes of the slice: x: 2, y: 2, z: 4, core: 2. Of those that a mesh axis runs over, the one named last changes fastest.
Arguments:
- init_state: float32 [512, 512], P('space'), may hold values from -6 to 6
- guess: float32 [4, 512, 512], P('tm', 'space'), may hold values from -6 to 6
- source: float32 [4, 2, 512, 512], P('tm', None, 'space'), may hold values from -6 to 6
- remap: int32 [512], P('space'), may hold values from 0 to 511, as said below
- neighbors: int32 [512, 6], P('space'), may hold values from -1 to 511, as said below
- block_class: int32 [512], P('space'), may hold values from 0 to 3
- step_number: float32 [4], replicated, may hold values from 0.3 to 3
- coarse_inverse: float32 [4, 64, 64], replicated, may hold values from -0.02 to 0.9
- coarse_step: float32 [4, 64, 64], replicated, may hold values from -0.02 to 0.99
Outputs:
- c_states: float32 [4, 512, 512], P('tm', 'space')
- f_states: float32 [4, 512, 512], P('tm', 'space')
Inputs may be any that keep to these rules, and one draw needn't show every extreme that they name: `remap`: the entries are a permutation of 0 to 511. The old blocks held by one device of space (aligned runs of 64) send at most 16 blocks to the new blocks held by any one device, and every device sends exactly 16 to some device. `neighbors`: entry [b, f] is the block beside block b across face f (the planes x = 0, x = 7, y = 0, y = 7, z = 0, z = 7 of the block), or -1 at the domain's boundary or at a wall. Links are mutual. Across faces 0 to 3 the neighbour lies in the same aligned run of 64 blocks; across face 4 in the run before, across face 5 in the run after.
All inputs are finite; a program needn't handle non-finite values.
Results may differ from a plain program's by a relative error of at most 0.00018.
Values sent between devices are 32-bit elements; how exact they have to be, the bound alone decides.
A program may use at most 64 MiB of HBM per device.

v0:
```python
import functools

import jax
import jax.numpy as jnp
from jax import lax
from jax.experimental import pallas as pl
from jax.experimental.pallas import tpu as pltpu
from jax.sharding import PartitionSpec as P

CELLS = 512
COARSE = 64
CLASSES = 4
ITERS = 2
DAMP = 0.8
MESH = pl.DeviceIdType.MESH
F32 = jnp.float32
BF16 = jnp.bfloat16


def split(value):
    high = value.astype(BF16)
    return high, (value - high.astype(F32)).astype(BF16)


def dot(left, right):
    return jnp.dot(left, right, preferred_element_type=F32)


def roll(value, shift):
    shift = shift % 128
    return value if shift == 0 else pltpu.roll(value, shift, 1)


def iota(shape, dim):
    return lax.broadcasted_iota(jnp.int32, shape, dim)


def kernel(
    n_tm, n_sp, bk,
    init_ref, guess_ref, source_ref, remap_ref, nb_ref, class_ref, step_ref, inv_ref, cstep_ref,
    c_ref, f_ref,
    gb, ib, gr, ir, hs, hr, st, hand, cs, cr,
    ohl, oh4, oh5, rm, pm, mi, ms, xs, vs, zs, dif,
    gs_sem, gr_sem, is_sem, ir_sem, hs_sem, hr_sem, ts_sem, tr_sem, cs_sem, cr_sem,
):
    k = lax.axis_index("tm")
    s = lax.axis_index("space")
    nb = init_ref.shape[0]
    half = nb // 2
    rows = n_sp * bk
    bits = nb.bit_length() - 1
    steps = 4

    hr[...] = jnp.zeros_like(hr)
    barrier = pltpu.get_barrier_semaphore()
    for off in range(1, n_sp):
        pl.semaphore_signal(barrier, inc=1, device_id=(k, lax.rem(s + off, n_sp)), device_id_type=MESH)
    for off in range(1, n_tm):
        pl.semaphore_signal(barrier, inc=1, device_id=(lax.rem(k + off, n_tm), s), device_id_type=MESH)

    eye = iota((nb, nb), 0) == iota((nb, nb), 1)

    def column(row):
        return jnp.sum(jnp.where(eye, row, 0.0), axis=1, keepdims=True)

    remap_row = remap_ref[...]
    target_row = lax.shift_right_logical(remap_row, bits)
    slot_row = (remap_row - lax.shift_left(target_row, bits)).astype(F32)
    target_f = target_row.astype(F32)
    same = (column(target_f) == target_f) & (iota((nb, nb), 0) < iota((nb, nb), 1))
    pos_row = jnp.sum(jnp.where(same, 1.0, 0.0), axis=0, keepdims=True)
    send_row = target_f * float(bk) + pos_row
    chosen = iota((rows, nb), 0).astype(F32) == send_row
    send_mat = jnp.where(chosen, 1.0, 0.0)
    slot_col = jnp.sum(jnp.where(chosen, slot_row + 1.0, 0.0), axis=1, keepdims=True) - 1.0
    send_mat = jnp.concatenate([send_mat, send_mat], axis=1).astype(BF16)

    def bucketed(value):
        return dot(send_mat, jnp.concatenate(split(value), axis=0)).reshape(n_sp, bk, CELLS)

    gb[:, :, :CELLS] = bucketed(guess_ref[0])
    gb[:, :, CELLS:] = jnp.broadcast_to(slot_col, (rows, 128)).reshape(n_sp, bk, 128)

    pl.semaphore_wait(barrier, n_sp - 1 + n_tm - 1)

    def move(src, dst, ssem, rsem, off):
        to = lax.rem(s + off, n_sp)
        return pltpu.make_async_remote_copy(
            src_ref=src.at[to], dst_ref=dst.at[s], send_sem=ssem.at[off], recv_sem=rsem.at[s],
            device_id=(k, to), device_id_type=MESH)

    def landed(src, dst, ssem, rsem, off):
        origin = lax.rem(s - off + n_sp, n_sp)
        pltpu.make_async_remote_copy(
            src_ref=src.at[origin], dst_ref=dst.at[origin], send_sem=ssem.at[off],
            recv_sem=rsem.at[origin], device_id=(k, origin), device_id_type=MESH).wait_recv()

    for off in range(1, n_sp):
        move(gb, gr, gs_sem, gr_sem, off).start()
    gr[s] = gb[s]

    @pl.when(k == 0)
    def _():
        ib[...] = bucketed(init_ref[...])
        for off in range(1, n_sp):
            move(ib, ir, is_sem, ir_sem, off).start()
        ir[s] = ib[s]

    class_col = column(class_ref[...].astype(F32))
    diffusion = jnp.zeros((nb, 1), F32)
    for cl in range(CLASSES):
        diffusion = diffusion + jnp.where(class_col == float(cl), step_ref[:, cl:cl + 1], 0.0)
    dif[...] = jnp.broadcast_to(diffusion, (nb, 128))

    lane_nb = iota((nb, nb), 1)
    for face in range(6):
        shift = s * nb + (0 if face < 4 else (-nb if face == 4 else nb))
        ids = nb_ref[:, face:face + 1]
        hot = jnp.where((ids - shift == lane_nb) & (ids >= 0), 1.0, 0.0)
        hot = jnp.concatenate([hot, hot], axis=1).astype(BF16)
        if face < 4:
            ohl[face * nb:(face + 1) * nb] = hot
        elif face == 4:
            oh4[...] = hot
        else:
            oh5[...] = hot

    def parent(cell):
        return (lax.shift_right_logical(cell, 7) * 16
                + (lax.shift_right_logical(cell, 4) & 3) * 4
                + lax.shift_right_logical(cell & 7, 1))

    rm[...] = jnp.where(parent(iota((CELLS, 128), 0)) == iota((CELLS, 128), 1), 0.125, 0.0).astype(BF16)
    pm[...] = jnp.where(parent(iota((128, CELLS), 1)) == (iota((128, CELLS), 0) & 63), 1.0, 0.0).astype(BF16)
    for src, dst in ((inv_ref, mi), (cstep_ref, ms)):
        high, low = split(src[...].T)
        dst[...] = jnp.concatenate([high, high, low, jnp.zeros_like(low)], axis=0)

    lane = iota((nb, 128), 1)
    zz = lane & 7
    yy = lax.shift_right_logical(lane, 3) & 7
    left = lane < 64
    zh = zz[:half]

    def classes(coarse, mat):
        high = coarse.astype(BF16).astype(F32)
        both = high + roll(coarse - high, 64)
        product = dot(jnp.concatenate([both, high], axis=1).astype(BF16), mat[...])
        low_c = jnp.where(left, 0.0, 1.0)
        picked = (jnp.where(class_col == low_c, product[:, :128], 0.0)
                  + jnp.where(class_col == low_c + 2.0, product[:, 128:], 0.0))
        return jnp.where(left, picked + roll(picked, 64), 0.0)

    def prolong(coarse):
        high = coarse.astype(BF16).astype(F32)
        return dot((high + roll(coarse - high, 64)).astype(BF16), pm[...])

    def restrict(value):
        both = dot(jnp.concatenate(split(value), axis=0), rm[...])
        return both[:nb] + both[nb:]

    def halo_up(slot):
        return pltpu.make_async_remote_copy(
            src_ref=hs.at[slot, 0], dst_ref=hr.at[slot, 0], send_sem=hs_sem.at[slot, 0],
            recv_sem=hr_sem.at[slot, 0], device_id=(k, lax.rem(s + 1, n_sp)), device_id_type=MESH)

    def halo_down(slot):
        return pltpu.make_async_remote_copy(
            src_ref=hs.at[slot, 1], dst_ref=hr.at[slot, 1], send_sem=hs_sem.at[slot, 1],
            recv_sem=hr_sem.at[slot, 1], device_id=(k, lax.rem(s + n_sp - 1, n_sp)), device_id_type=MESH)

    def tiles_of(value):
        return [value[:, 128 * j:128 * j + 128] for j in range(4)]

    def beside(value, slot):
        tiles = tiles_of(value)
        top = bottom = jnp.zeros((nb, 128), F32)
        for j in range(4):
            top = jnp.where(zz == j, roll(tiles[j], j - 7), top)
            bottom = jnp.where(zz == j, roll(tiles[j], j), bottom)
        hs[slot, 0] = jnp.where(zh < 4, top[:half], roll(top[half:], 4))
        hs[slot, 1] = jnp.where(zh < 4, bottom[:half], roll(bottom[half:], 4))

        @pl.when(s < n_sp - 1)
        def _():
            halo_up(slot).start()

        @pl.when(s > 0)
        def _():
            halo_down(slot).start()

        xface = jnp.where(left, roll(tiles[3], 64), roll(tiles[0], 64))
        yface = jnp.zeros((nb, 128), F32)
        for j in range(4):
            yface = jnp.where(yy == j, roll(tiles[j], 8 * j - 56), yface)
            yface = jnp.where(yy == 4 + j, roll(tiles[j], 32 + 8 * j), yface)
        ghosts = dot(ohl[...], jnp.concatenate(split(jnp.concatenate([xface, yface], axis=1)), axis=0))
        turned = [roll(tile, 64) for tile in tiles]
        turned = [ghosts[:nb, :128]] + turned + [ghosts[nb:2 * nb, :128]]
        g2 = ghosts[2 * nb:3 * nb, 128:]
        g3 = ghosts[3 * nb:, 128:]
        sums = []
        for j in range(4):
            total = turned[j + 1] + jnp.where(left, turned[j], turned[j + 2])
            total = total + jnp.where(yy == 0, roll(g2, -8 * j), roll(tiles[j], 8))
            total = total + jnp.where(yy == 7, roll(g3, 24 - 8 * j), roll(tiles[j], -8))
            total = total + jnp.where(zz == 0, 0.0, roll(tiles[j], 1))
            total = total + jnp.where(zz == 7, 0.0, roll(tiles[j], -1))
            sums.append(total)

        @pl.when(s > 0)
        def _():
            halo_up(slot).wait_recv()

        @pl.when(s < n_sp - 1)
        def _():
            halo_down(slot).wait_recv()

        def across(packed, hot):
            both = jnp.concatenate([packed, roll(packed, -4)], axis=0)
            return dot(hot[...], jnp.concatenate(split(both), axis=0))

        g4 = across(hr[slot, 0], oh4)
        g5 = across(hr[slot, 1], oh5)
        for j in range(4):
            sums[j] = (sums[j] + jnp.where(zz == 0, roll(g4, -j), 0.0)
                       + jnp.where(zz == 7, roll(g5, 7 - j), 0.0))
        return jnp.concatenate(sums, axis=1)

    def wide():
        diffused = jnp.concatenate([dif[...]] * 4, axis=1)
        return diffused, 1.0 + 6.0 * diffused

    def leftover(value, slot):
        diffused, diagonal = wide()
        return vs[...] - (diagonal * value - diffused * beside(value, slot))

    def sweep(slot):
        value = xs[...]
        rest = leftover(value, slot)
        xs[...] = value + DAMP * rest / wide()[1]

    def vcycle(base):
        xs[...] = DAMP * vs[...] / wide()[1]
        sweep(base)
        value = xs[...]
        rest = leftover(value, base + 1)
        xs[...] = value + prolong(classes(restrict(rest), mi))
        lax.fori_loop(0, 2, lambda i, c: (sweep(base + 2 + i), c)[1], 0)

    for off in range(1, n_sp):
        landed(gb, gr, gs_sem, gr_sem, off)
    arrived = gr[...].reshape(rows, CELLS + 128)
    slots = arrived[:, CELLS:CELLS + nb]
    take = jnp.where(slots == iota((rows, nb), 1).astype(F32), 1.0, 0.0).T.astype(BF16)

    def settled(value):
        high, low = split(value)
        return dot(take, high) + dot(take, low)

    st[0] = settled(arrived[:, :CELLS])

    def hand_copy(it):
        return pltpu.make_async_remote_copy(
            src_ref=st.at[it], dst_ref=hand.at[it], send_sem=ts_sem.at[it], recv_sem=tr_sem.at[it],
            device_id=(lax.rem(k + 1, n_tm), s), device_id_type=MESH)

    def coarse_copy(it, off):
        return pltpu.make_async_remote_copy(
            src_ref=cs.at[it], dst_ref=cr.at[it, k], send_sem=cs_sem.at[it, off],
            recv_sem=cr_sem.at[it, k], device_id=(lax.rem(k + off, n_tm), s), device_id_type=MESH)

    def coarse_landed(it, origin):
        pltpu.make_async_remote_copy(
            src_ref=cs.at[it], dst_ref=cr.at[it, origin], send_sem=cs_sem.at[it, 0],
            recv_sem=cr_sem.at[it, origin], device_id=(lax.rem(k + 1, n_tm), s),
            device_id_type=MESH).wait_recv()

    def iteration(it, carry):
        @pl.when(k < n_tm - 1)
        def _():
            hand_copy(it).start()

        @pl.when((k == 0) & (it == 0))
        def _():
            for off in range(1, n_sp):
                landed(ib, ir, is_sem, ir_sem, off)
            start = settled(ir[...].reshape(rows, CELLS))
            for i in range(ITERS):
                hand[i] = start

        @pl.when(k > 0)
        def _():
            hand_copy(it).wait_recv()

        vs[...] = hand[it] + source_ref[0, 0]

        def one(v, c):
            vcycle((it * 2 + v) * steps)

            @pl.when(v == 0)
            def _():
                f_ref[0] = xs[...]
                vs[...] = xs[...] + source_ref[0, 1]
            return c

        lax.fori_loop(0, 2, one, 0)
        residual = xs[...] - st[it]
        cs[it] = restrict(residual)
        for off in range(1, n_tm):
            @pl.when(k + off < n_tm)
            def _():
                coarse_copy(it, off).start()
        zs[...] = jnp.zeros_like(zs)
        for j in range(n_tm - 1):
            @pl.when(j < k)
            def _():
                coarse_landed(it, j)
                zs[...] = classes(zs[...], ms) + cr[it, j]
        st[it + 1] = st[it] + (prolong(classes(zs[...], ms)) + residual)
        return carry

    lax.fori_loop(0, ITERS, iteration, 0)
    c_ref[0] = st[ITERS]

    for off in range(1, n_sp):
        move(gb, gr, gs_sem, gr_sem, off).wait_send()

    @pl.when(k == 0)
    def _():
        for off in range(1, n_sp):
            move(ib, ir, is_sem, ir_sem, off).wait_send()

    def drain(slot, carry):
        @pl.when(s < n_sp - 1)
        def _():
            halo_up(slot).wait_send()

        @pl.when(s > 0)
        def _():
            halo_down(slot).wait_send()
        return carry

    lax.fori_loop(0, ITERS * 2 * steps, drain, 0)
    for it in range(ITERS):
        @pl.when(k < n_tm - 1)
        def _():
            hand_copy(it).wait_send()
        for off in range(1, n_tm):
            @pl.when(k + off < n_tm)
            def _():
                coarse_copy(it, off).wait_send()


def solution(mesh):
    n_tm, n_sp = mesh.shape["tm"], mesh.shape["space"]

    def body(init_state, guess, source, remap, neighbors, block_class, step_number, inverse, cstep):
        nb = init_state.shape[0]
        bk = -(-(2 * nb // n_sp) // 8) * 8
        slots = ITERS * 2 * 4
        dma = pltpu.SemaphoreType.DMA
        out = jax.ShapeDtypeStruct((1, nb, CELLS), F32)
        return pl.pallas_call(
            functools.partial(kernel, n_tm, n_sp, bk),
            name="mgrit",
            out_shape=(out, out),
            in_specs=[pl.BlockSpec(memory_space=pltpu.VMEM)] * 9,
            out_specs=[pl.BlockSpec(memory_space=pltpu.VMEM)] * 2,
            scratch_shapes=[
                pltpu.VMEM((n_sp, bk, CELLS + 128), F32),
                pltpu.VMEM((n_sp, bk, CELLS), F32),
                pltpu.VMEM((n_sp, bk, CELLS + 128), F32),
                pltpu.VMEM((n_sp, bk, CELLS), F32),
                pltpu.VMEM((slots, 2, nb // 2, 128), F32),
                pltpu.VMEM((slots, 2, nb // 2, 128), F32),
                pltpu.VMEM((ITERS + 1, nb, CELLS), F32),
                pltpu.VMEM((ITERS, nb, CELLS), F32),
                pltpu.VMEM((ITERS, nb, 128), F32),
                pltpu.VMEM((ITERS, n_tm, nb, 128), F32),
                pltpu.VMEM((4 * nb, 2 * nb), BF16),
                pltpu.VMEM((nb, 2 * nb), BF16),
                pltpu.VMEM((nb, 2 * nb), BF16),
                pltpu.VMEM((CELLS, 128), BF16),
                pltpu.VMEM((128, CELLS), BF16),
                pltpu.VMEM((4 * COARSE, CLASSES * COARSE), BF16),
                pltpu.VMEM((4 * COARSE, CLASSES * COARSE), BF16),
                pltpu.VMEM((nb, CELLS), F32),
                pltpu.VMEM((nb, CELLS), F32),
                pltpu.VMEM((nb, 128), F32),
                pltpu.VMEM((nb, 128), F32),
                dma((n_sp,)), dma((n_sp,)), dma((n_sp,)), dma((n_sp,)),
                dma((slots, 2)), dma((slots, 2)),
                dma((ITERS,)), dma((ITERS,)),
                dma((ITERS, n_tm)), dma((ITERS, n_tm)),
            ],
            compiler_params=pltpu.CompilerParams(collective_id=0, has_side_effects=True),
        )(
            init_state, guess, source, remap.reshape(1, nb), neighbors, block_class.reshape(1, nb),
            step_number.reshape(1, CLASSES), inverse.reshape(CLASSES * COARSE, COARSE),
            cstep.reshape(CLASSES * COARSE, COARSE),
        )

    placed = (
        P("space", None), P("tm", "space", None), P("tm", None, "space", None), P("space"),
        P("space", None), P("space"), P(), P(), P(),
    )
    return jax.shard_map(
        body, mesh=mesh, in_specs=placed,
        out_specs=(P("tm", "space", None), P("tm", "space", None)), check_vma=False,
    )
```

profile of v0, /device:TPU:14, one launch (start us, length us, event | category | flops | bytes accessed | tf_op | source)
XLA Modules:
  0.0 84.7 jit_solution(6831928127032834061)
XLA Ops:
  0.6 0.0 copy-start.1
  0.6 0.7 copy-done.1
  1.3 0.7 copy.11.nb_ref
  2.0 80.4 %mgrit.1 = (f32[1,64,512]{2,1,0:T(8,128)}, f32[1,64,512]{2,1,0:T(8,128)}) custom-call(f32[64,512]{1,0:T(8,128)} %init_ref.1, f32[1,64,512]{2,1,0:T(8,128)} %guess_ref.1, f32[1,2,64,512]{3,2,1,0:T(8,128)} %source_ref.1, s32[1,64]{1,0:T(1,128)} %bitcast.7, s32[64,6]{1,0:T(8,128)} %copy.11.nb_ref, s32[1,64]{1,0:T(1,128)} %bitcast.8, f32[1,4]{1,0:T(1,128)} %bitcast.9, ...), custom_call_target="tpu_custom_call" | custom-call | tf_op jit(solution)/shard_map/mgrit/pallas_call | solution.py:364
  82.5 0.0 copy-start
  82.5 1.6 %copy.14 = f32[1,64,512]{2,1,0:T(8,128)} copy(f32[1,64,512]{2,1,0:T(8,128)} %get-tuple-element.4) | data formatting | bytes 262144
  84.1 0.0 copy-done
  84.1 0.7 copy.15
Async XLA Ops:
  0.6 0.7 copy-start.1
  82.5 1.6 %copy-start = (f32[1,64,512]{2,1,0:T(8,128)S(1)}, f32[1,64,512]{2,1,0:T(8,128)}, u32[]{:S(2)}) copy-start(f32[1,64,512]{2,1,0:T(8,128)} %get-tuple-element.5) | copy-start | bytes 393220
where the time goes:
time: 84.9 us; the launch traced here: 84.7 us
  Pallas kernels  80.4 us (95%)
  local copies, waits for them, and re-layouts  3.65 us (4%)
    pallas_call x1, Pallas kernels, body(): pl.pallas_call(functools.partial(kernel, n_tm, n_sp, bk), name='mgrit', o...  80.4 us
    unnamed x7, local copies, waits for them, and re-layouts  3.65 us

commit v1 on v0

v1 whole, which is shorter than its diff:
```python
import functools

import jax
import jax.numpy as jnp
from jax import lax
from jax.experimental import pallas as pl
from jax.experimental.pallas import tpu as pltpu
from jax.sharding import PartitionSpec as P

CELLS = 512
COARSE = 64
CLASSES = 4
ITERS = 2
DAMP = 0.8
MESH = pl.DeviceIdType.MESH
F32 = jnp.float32
BF16 = jnp.bfloat16


def split(value):
    high = value.astype(BF16)
    return high, (value - high.astype(F32)).astype(BF16)


def dot(left, right):
    return jnp.dot(left, right, preferred_element_type=F32)


def roll(value, shift):
    shift = shift % 128
    return value if shift == 0 else pltpu.roll(value, shift, 1)


def iota(shape, dim):
    return lax.broadcasted_iota(jnp.int32, shape, dim)


def kernel(
    n_tm, n_sp, bk,
    init_ref, guess_ref, source_ref, remap_ref, nb_ref, class_ref, step_ref, inv_ref, cstep_ref,
    c_ref, f_ref,
    gb, ib, gr, br, hs, hr, st, hsrc, hand, cs, cr,
    ohl, ohn, oh4, oh5, oh4t, oh5t, rm, pm, mi, ms, xs, ws, bs, zs, ps, scale, near,
    gs_sem, gr_sem, ps_sem, is_sem, br_sem, hs_sem, hr_sem, ts_sem, tr_sem, cs_sem, cr_sem,
):
    k = lax.axis_index("tm")
    s = lax.axis_index("space")
    nb = init_ref.shape[0]
    rows = n_sp * bk
    bits = nb.bit_length() - 1
    setup = ITERS * 4

    hr[...] = jnp.zeros_like(hr)
    barrier = pltpu.get_barrier_semaphore()
    for off in range(1, n_sp):
        pl.semaphore_signal(barrier, inc=1, device_id=(k, lax.rem(s + off, n_sp)), device_id_type=MESH)
    for off in range(1, n_tm):
        pl.semaphore_signal(barrier, inc=1, device_id=(lax.rem(k + off, n_tm), s), device_id_type=MESH)

    @pl.when(k < n_tm - 1)
    def _():
        for off in range(1, n_sp):
            pl.semaphore_signal(barrier, inc=1, device_id=(k + 1, lax.rem(s + off, n_sp)), device_id_type=MESH)

    @pl.when(k > 0)
    def _():
        for off in range(1, n_sp):
            pl.semaphore_signal(barrier, inc=1, device_id=(k - 1, lax.rem(s + off, n_sp)), device_id_type=MESH)

    eye = iota((nb, nb), 0) == iota((nb, nb), 1)

    def column(row):
        return jnp.sum(jnp.where(eye, row, 0.0), axis=1, keepdims=True)

    remap_row = remap_ref[...]
    target_row = lax.shift_right_logical(remap_row, bits)
    slot_row = (remap_row - lax.shift_left(target_row, bits)).astype(F32)
    target_f = target_row.astype(F32)
    same = (column(target_f) == target_f) & (iota((nb, nb), 0) < iota((nb, nb), 1))
    pos_row = jnp.sum(jnp.where(same, 1.0, 0.0), axis=0, keepdims=True)
    send_row = target_f * float(bk) + pos_row
    chosen = iota((rows, nb), 0).astype(F32) == send_row
    send_mat = jnp.where(chosen, 1.0, 0.0)
    slot_col = jnp.sum(jnp.where(chosen, slot_row + 1.0, 0.0), axis=1, keepdims=True) - 1.0
    send_mat = jnp.concatenate([send_mat, send_mat], axis=1).astype(BF16)

    def bucketed(value):
        return dot(send_mat, jnp.concatenate(split(value), axis=0)).reshape(n_sp, bk, CELLS)

    slot_tile = jnp.broadcast_to(slot_col, (rows, 128)).reshape(n_sp, bk, 128)
    gb[:, :, :CELLS] = bucketed(guess_ref[0])
    gb[:, :, CELLS:] = slot_tile

    @pl.when(k == 0)
    def _():
        ib[:, :, :CELLS] = bucketed(init_ref[...])
        ib[:, :, CELLS:] = slot_tile

    sides = jnp.minimum(k, 1) + jnp.minimum(n_tm - 1 - k, 1)
    pl.semaphore_wait(barrier, (n_sp - 1) * (1 + sides) + n_tm - 1)

    def spread_copy(src, ssem, off, col):
        to = lax.rem(s + off, n_sp)
        return pltpu.make_async_remote_copy(
            src_ref=src.at[to], dst_ref=br.at[s], send_sem=ssem.at[off], recv_sem=br_sem.at[s],
            device_id=(col, to), device_id_type=MESH)

    def own_copy(off):
        to = lax.rem(s + off, n_sp)
        return pltpu.make_async_remote_copy(
            src_ref=gb.at[to, :, pl.ds(0, CELLS)], dst_ref=gr.at[s], send_sem=gs_sem.at[off],
            recv_sem=gr_sem.at[s], device_id=(k, to), device_id_type=MESH)

    def spread_landed(off):
        origin = lax.rem(s + off, n_sp)
        pltpu.make_async_remote_copy(
            src_ref=gb.at[origin], dst_ref=br.at[origin], send_sem=ps_sem.at[off],
            recv_sem=br_sem.at[origin], device_id=(lax.rem(k + 1, n_tm), origin),
            device_id_type=MESH).wait_recv()

    def own_landed(off):
        origin = lax.rem(s + off, n_sp)
        pltpu.make_async_remote_copy(
            src_ref=gb.at[origin, :, pl.ds(0, CELLS)], dst_ref=gr.at[origin],
            send_sem=gs_sem.at[off], recv_sem=gr_sem.at[origin], device_id=(k, origin),
            device_id_type=MESH).wait_recv()

    @pl.when(k == 0)
    def _():
        for off in range(1, n_sp):
            spread_copy(ib, is_sem, off, k).start()
        br[s] = ib[s]

    @pl.when(k < n_tm - 1)
    def _():
        for off in range(n_sp):
            spread_copy(gb, ps_sem, off, lax.rem(k + 1, n_tm)).start()

    class_col = column(class_ref[...].astype(F32))
    diffusion = jnp.zeros((nb, 1), F32)
    for cl in range(CLASSES):
        diffusion = diffusion + jnp.where(class_col == float(cl), step_ref[:, cl:cl + 1], 0.0)
    dif = jnp.broadcast_to(diffusion, (nb, 128))
    scale[0] = DAMP * dif / (1.0 + 6.0 * dif)
    scale[1] = DAMP / (1.0 + 6.0 * dif)
    scale[2] = (1.0 + 6.0 * dif) / DAMP
    lane = iota((nb, 128), 1)
    table = jnp.where(lane == 4, dif, -1.0)
    for face in range(4):
        table = jnp.where(lane == face, (nb_ref[:, face:face + 1] - s * nb).astype(F32), table)
    hs[setup, 0] = table
    hs[setup, 1] = table

    def halo_up(slot):
        return pltpu.make_async_remote_copy(
            src_ref=hs.at[slot, 0], dst_ref=hr.at[slot, 0], send_sem=hs_sem.at[slot, 0],
            recv_sem=hr_sem.at[slot, 0], device_id=(k, lax.rem(s + 1, n_sp)), device_id_type=MESH)

    def halo_down(slot):
        return pltpu.make_async_remote_copy(
            src_ref=hs.at[slot, 1], dst_ref=hr.at[slot, 1], send_sem=hs_sem.at[slot, 1],
            recv_sem=hr_sem.at[slot, 1], device_id=(k, lax.rem(s + n_sp - 1, n_sp)), device_id_type=MESH)

    def exchange(slot):
        @pl.when(s < n_sp - 1)
        def _():
            halo_up(slot).start()

        @pl.when(s > 0)
        def _():
            halo_down(slot).start()

    def exchanged(slot):
        @pl.when(s > 0)
        def _():
            halo_up(slot).wait_recv()

        @pl.when(s < n_sp - 1)
        def _():
            halo_down(slot).wait_recv()

    exchange(setup)
    for off in range(1, n_sp):
        own_copy(off).start()
    gr[s] = gb[s, :, :CELLS]

    lane_nb = iota((nb, nb), 1)
    for face in range(6):
        shift = s * nb + (0 if face < 4 else (-nb if face == 4 else nb))
        ids = nb_ref[:, face:face + 1]
        hot = jnp.where((ids - shift == lane_nb) & (ids >= 0), 1.0, 0.0)
        if face >= 4:
            turned = hot.T
            turned = jnp.concatenate([turned, turned], axis=1).astype(BF16)
            (oh4t if face == 4 else oh5t)[...] = turned
        hot = jnp.concatenate([hot, hot], axis=1).astype(BF16)
        if face < 4:
            ohl[face * nb:(face + 1) * nb] = hot
        elif face == 4:
            oh4[...] = hot
        else:
            oh5[...] = hot

    def parent(cell):
        return (lax.shift_right_logical(cell, 7) * 16
                + (lax.shift_right_logical(cell, 4) & 3) * 4
                + lax.shift_right_logical(cell & 7, 1))

    rm[...] = jnp.where(parent(iota((CELLS, 128), 0)) == iota((CELLS, 128), 1), 0.125, 0.0).astype(BF16)
    pm[...] = jnp.where(parent(iota((128, CELLS), 1)) == (iota((128, CELLS), 0) & 63), 1.0, 0.0).astype(BF16)
    for src, dst in ((inv_ref, mi), (cstep_ref, ms)):
        high, low = split(src[...].T)
        dst[...] = jnp.concatenate([high, high, low, jnp.zeros_like(low)], axis=0)

    zz = lane & 7
    yy = lax.shift_right_logical(lane, 3) & 7
    left = lane < 64

    def classes(coarse, mat):
        high = coarse.astype(BF16).astype(F32)
        both = high + roll(coarse - high, 64)
        product = dot(jnp.concatenate([both, high], axis=1).astype(BF16), mat[...])
        low_c = jnp.where(left, 0.0, 1.0)
        picked = (jnp.where(class_col == low_c, product[:, :128], 0.0)
                  + jnp.where(class_col == low_c + 2.0, product[:, 128:], 0.0))
        return jnp.where(left, picked + roll(picked, 64), 0.0)

    def prolong(coarse):
        high = coarse.astype(BF16).astype(F32)
        return dot((high + roll(coarse - high, 64)).astype(BF16), pm[...])

    def restrict(value):
        both = dot(jnp.concatenate(split(value), axis=0), rm[...])
        return both[:nb] + both[nb:]

    def tiles_of(value):
        return [value[:, 128 * j:128 * j + 128] for j in range(4)]

    def gathered(hot, value):
        return dot(hot, jnp.concatenate(split(value), axis=0))

    def planes(tiles):
        top = bottom = jnp.zeros((nb, 128), F32)
        for j in range(4):
            top = jnp.where(zz == j, roll(tiles[j], j - 7), top)
            top = jnp.where(zz == 4 + j, roll(tiles[j], j - 2), top)
            bottom = jnp.where(zz == j, roll(tiles[j], j), bottom)
            bottom = jnp.where(zz == 4 + j, roll(tiles[j], j + 3), bottom)
        return top, bottom

    def plane_step(plane, driven, side, cross):
        w = gathered(ohn[side], plane)
        turned = roll(plane, 64)
        total = turned + jnp.where(
            left, jnp.where(zz == 0, roll(w[:nb], -67), roll(turned, 1)),
            jnp.where(zz == 3, roll(w[nb:2 * nb], 67), roll(turned, -1)))
        total = total + jnp.where(yy == 0, roll(w[2 * nb:3 * nb], -56), roll(plane, 8))
        total = total + jnp.where(yy == 7, roll(w[3 * nb:], 56), roll(plane, -8))
        total = total + roll(plane, -4) + cross
        return (1.0 - DAMP) * plane + driven + near[side] * total

    def inside(tiles):
        xface = jnp.where(left, roll(tiles[3], 64), roll(tiles[0], 64))
        yface = jnp.zeros((nb, 128), F32)
        for j in range(4):
            yface = jnp.where(yy == j, roll(tiles[j], 8 * j - 56), yface)
            yface = jnp.where(yy == 4 + j, roll(tiles[j], 32 + 8 * j), yface)
        ghosts = gathered(ohl[...], jnp.concatenate([xface, yface], axis=1))
        turned = [roll(tile, 64) for tile in tiles]
        turned = [ghosts[:nb, :128]] + turned + [ghosts[nb:2 * nb, :128]]
        g2 = ghosts[2 * nb:3 * nb, 128:]
        g3 = ghosts[3 * nb:, 128:]
        sums = []
        for j in range(4):
            total = turned[j + 1] + jnp.where(left, turned[j], turned[j + 2])
            total = total + jnp.where(yy == 0, roll(g2, -8 * j), roll(tiles[j], 8))
            total = total + jnp.where(yy == 7, roll(g3, 24 - 8 * j), roll(tiles[j], -8))
            total = total + jnp.where(zz == 0, 0.0, roll(tiles[j], 1))
            total = total + jnp.where(zz == 7, 0.0, roll(tiles[j], -1))
            sums.append(total)
        return sums

    def with_ends(sums, below, above):
        g4 = gathered(oh4[...], below)
        g5 = gathered(oh5[...], above)
        return [
            sums[j] + jnp.where(zz == 0, roll(g4, -j), 0.0) + jnp.where(zz == 7, roll(g5, 7 - j), 0.0)
            for j in range(4)
        ]

    def swept(tiles, driven, sums):
        return [(1.0 - DAMP) * tiles[j] + driven[j] + scale[0] * sums[j] for j in range(4)]

    def vcycle(base):
        driven = tiles_of(ws[...])
        for stage in range(2):
            slot = base + stage
            tiles = driven if stage == 0 else tiles_of(xs[...])
            top, bottom = planes(tiles)
            hs[slot, 0] = top
            hs[slot, 1] = bottom
            exchange(slot)
            sums = inside(tiles)
            up_cross = gathered(oh4t[...], bottom)
            down_cross = gathered(oh5t[...], top)
            exchanged(slot)
            below, above = hr[slot, 0], hr[slot, 1]
            tiles = swept(tiles, driven, with_ends(sums, below, above))
            below = plane_step(below, hr[base, 0], 0, up_cross)
            above = plane_step(above, hr[base, 1], 1, down_cross)
            sums = with_ends(inside(tiles), below, above)
            if stage == 0:
                rest = jnp.concatenate(
                    [driven[j] - DAMP * tiles[j] + scale[0] * sums[j] for j in range(4)], axis=1)
                fix = prolong(classes(scale[2] * restrict(rest), mi))
                xs[...] = jnp.concatenate(tiles, axis=1) + fix
            else:
                xs[...] = jnp.concatenate(swept(tiles, driven, sums), axis=1)

    def drive(value):
        ws[...] = value * jnp.concatenate([scale[1]] * 4, axis=1)

    exchanged(setup)
    for side in range(2):
        table = hr[setup, side]
        far = table[:, 4:5]
        near[side] = jnp.broadcast_to(DAMP * far / (1.0 + 6.0 * far), (nb, 128))
        for face in range(4):
            hot = jnp.where(table[:, face:face + 1] == lane_nb.astype(F32), 1.0, 0.0)
            ohn[side, face * nb:(face + 1) * nb] = jnp.concatenate([hot, hot], axis=1).astype(BF16)

    for off in range(1, n_sp):
        spread_landed(off)

    @pl.when(k > 0)
    def _():
        spread_landed(0)

    arrived = br[...].reshape(rows, CELLS + 128)
    slots = arrived[:, CELLS:CELLS + nb]
    take = jnp.where(slots == iota((rows, nb), 1).astype(F32), 1.0, 0.0).T.astype(BF16)

    def settled(value):
        high, low = split(value)
        return dot(take, high) + dot(take, low)

    bs[...] = settled(arrived[:, :CELLS])

    def hand_copy(it):
        return pltpu.make_async_remote_copy(
            src_ref=hsrc.at[it], dst_ref=hand.at[it], send_sem=ts_sem.at[it], recv_sem=tr_sem.at[it],
            device_id=(lax.rem(k + 1, n_tm), s), device_id_type=MESH)

    def coarse_copy(it, off):
        return pltpu.make_async_remote_copy(
            src_ref=cs.at[it], dst_ref=cr.at[it, k], send_sem=cs_sem.at[it, off],
            recv_sem=cr_sem.at[it, k], device_id=(lax.rem(k + off, n_tm), s), device_id_type=MESH)

    def coarse_landed(it, origin):
        pltpu.make_async_remote_copy(
            src_ref=cs.at[it], dst_ref=cr.at[it, origin], send_sem=cs_sem.at[it, 0],
            recv_sem=cr_sem.at[it, origin], device_id=(lax.rem(k + 1, n_tm), s),
            device_id_type=MESH).wait_recv()

    def iteration(it, carry):
        drive(bs[...] + source_ref[0, 0])

        def one(v, c):
            vcycle((it * 2 + v) * 2)

            @pl.when(v == 0)
            def _():
                f_ref[0] = xs[...]
                drive(xs[...] + source_ref[0, 1])
            return c

        lax.fori_loop(0, 2, one, 0)

        @pl.when(it == 0)
        def _():
            for off in range(1, n_sp):
                own_landed(off)
            st[0] = settled(gr[...].reshape(rows, CELLS))

        residual = xs[...] - st[it]
        cs[it] = restrict(residual)
        for off in range(1, n_tm):
            @pl.when(k + off < n_tm)
            def _():
                coarse_copy(it, off).start()

        @pl.when((k < n_tm - 1) & (it < ITERS - 1))
        def _():
            hsrc[it] = xs[...]
            hand_copy(it).start()

        zs[...] = jnp.zeros_like(zs)
        ps[...] = jnp.zeros_like(ps)
        for j in range(n_tm - 1):
            @pl.when(j < k)
            def _():
                coarse_landed(it, j)
                pushed = classes(zs[...], ms)
                ps[...] = pushed
                zs[...] = pushed + cr[it, j]
        st[it + 1] = st[it] + (prolong(classes(zs[...], ms)) + residual)

        @pl.when((k > 0) & (it < ITERS - 1))
        def _():
            hand_copy(it).wait_recv()
            bs[...] = hand[it] + prolong(ps[...])
        return carry

    lax.fori_loop(0, ITERS, iteration, 0)
    c_ref[0] = st[ITERS]

    for off in range(1, n_sp):
        own_copy(off).wait_send()

    @pl.when(k == 0)
    def _():
        for off in range(1, n_sp):
            spread_copy(ib, is_sem, off, k).wait_send()

    @pl.when(k < n_tm - 1)
    def _():
        for off in range(n_sp):
            spread_copy(gb, ps_sem, off, lax.rem(k + 1, n_tm)).wait_send()

    def drain(slot, carry):
        @pl.when(s < n_sp - 1)
        def _():
            halo_up(slot).wait_send()

        @pl.when(s > 0)
        def _():
            halo_down(slot).wait_send()
        return carry

    lax.fori_loop(0, setup + 1, drain, 0)
    for it in range(ITERS):
        if it < ITERS - 1:
            @pl.when(k < n_tm - 1)
            def _():
                hand_copy(it).wait_send()
        for off in range(1, n_tm):
            @pl.when(k + off < n_tm)
            def _():
                coarse_copy(it, off).wait_send()


def solution(mesh):
    n_tm, n_sp = mesh.shape["tm"], mesh.shape["space"]

    def body(init_state, guess, source, remap, neighbors, block_class, step_number, inverse, cstep):
        nb = init_state.shape[0]
        bk = -(-(2 * nb // n_sp) // 8) * 8
        slots = ITERS * 4 + 1
        dma = pltpu.SemaphoreType.DMA
        out = jax.ShapeDtypeStruct((1, nb, CELLS), F32)
        return pl.pallas_call(
            functools.partial(kernel, n_tm, n_sp, bk),
            name="mgrit",
            out_shape=(out, out),
            in_specs=[pl.BlockSpec(memory_space=pltpu.VMEM)] * 9,
            out_specs=[pl.BlockSpec(memory_space=pltpu.VMEM)] * 2,
            scratch_shapes=[
                pltpu.VMEM((n_sp, bk, CELLS + 128), F32),
                pltpu.VMEM((n_sp, bk, CELLS + 128), F32),
                pltpu.VMEM((n_sp, bk, CELLS), F32),
                pltpu.VMEM((n_sp, bk, CELLS + 128), F32),
                pltpu.VMEM((slots, 2, nb, 128), F32),
                pltpu.VMEM((slots, 2, nb, 128), F32),
                pltpu.VMEM((ITERS + 1, nb, CELLS), F32),
                pltpu.VMEM((ITERS, nb, CELLS), F32),
                pltpu.VMEM((ITERS, nb, CELLS), F32),
                pltpu.VMEM((ITERS, nb, 128), F32),
                pltpu.VMEM((ITERS, n_tm, nb, 128), F32),
                pltpu.VMEM((4 * nb, 2 * nb), BF16),
                pltpu.VMEM((2, 4 * nb, 2 * nb), BF16),
                pltpu.VMEM((nb, 2 * nb), BF16),
                pltpu.VMEM((nb, 2 * nb), BF16),
                pltpu.VMEM((nb, 2 * nb), BF16),
                pltpu.VMEM((nb, 2 * nb), BF16),
                pltpu.VMEM((CELLS, 128), BF16),
                pltpu.VMEM((128, CELLS), BF16),
                pltpu.VMEM((4 * COARSE, CLASSES * COARSE), BF16),
                pltpu.VMEM((4 * COARSE, CLASSES * COARSE), BF16),
                pltpu.VMEM((nb, CELLS), F32),
                pltpu.VMEM((nb, CELLS), F32),
                pltpu.VMEM((nb, CELLS), F32),
                pltpu.VMEM((nb, 128), F32),
                pltpu.VMEM((nb, 128), F32),
                pltpu.VMEM((3, nb, 128), F32),
                pltpu.VMEM((2, nb, 128), F32),
                dma((n_sp,)), dma((n_sp,)), dma((n_sp,)), dma((n_sp,)), dma((n_sp,)),
                dma((slots, 2)), dma((slots, 2)),
                dma((ITERS,)), dma((ITERS,)),
                dma((ITERS, n_tm)), dma((ITERS, n_tm)),
            ],
            compiler_params=pltpu.CompilerParams(collective_id=0, has_side_effects=True),
        )(
            init_state, guess, source, remap.reshape(1, nb), neighbors, block_class.reshape(1, nb),
            step_number.reshape(1, CLASSES), inverse.reshape(CLASSES * COARSE, COARSE),
            cstep.reshape(CLASSES * COARSE, COARSE),
        )

    placed = (
        P("space", None), P("tm", "space", None), P("tm", None, "space", None), P("space"),
        P("space", None), P("space"), P(), P(), P(),
    )
    return jax.shard_map(
        body, mesh=mesh, in_specs=placed,
        out_specs=(P("tm", "space", None), P("tm", "space", None)), check_vma=False,
    )
```

time: 84.9 us -> 71.9 us (0.85); the launches traced: 84.7 us -> 70.9 us
  Pallas kernels: 80.4 us -> 66.6 us
    pallas_call x1, Pallas kernels: 80.4 us -> 66.6 us  [body(): pl.pallas_call(functools.partial(kernel, n_tm, n_sp, bk), name='mgrit', o...]
where the time goes in v1:
time: 71.9 us; the launch traced here: 70.9 us
  Pallas kernels  66.6 us (93%)
  local copies, waits for them, and re-layouts  3.65 us (5%)
    pallas_call x1, Pallas kernels, body(): pl.pallas_call(functools.partial(kernel, n_tm, n_sp, bk), name='mgrit', o...  66.6 us
    unnamed x7, local copies, waits for them, and re-layouts  3.65 us

profile of v1, /device:TPU:14, one launch (start us, length us, event | category | flops | bytes accessed | tf_op | source)
XLA Modules:
  0.0 70.9 jit_solution(16973047050353878260)
XLA Ops:
  0.6 0.0 copy-start.1
  0.6 0.7 copy-done.1
  1.3 0.7 copy.11.nb_ref
  2.0 66.6 %mgrit.1 = (f32[1,64,512]{2,1,0:T(8,128)}, f32[1,64,512]{2,1,0:T(8,128)}) custom-call(f32[64,512]{1,0:T(8,128)} %init_ref.1, f32[1,64,512]{2,1,0:T(8,128)} %guess_ref.1, f32[1,2,64,512]{3,2,1,0:T(8,128)} %source_ref.1, s32[1,64]{1,0:T(1,128)} %bitcast.7, s32[64,6]{1,0:T(8,128)} %copy.11.nb_ref, s32[1,64]{1,0:T(1,128)} %bitcast.8, f32[1,4]{1,0:T(1,128)} %bitcast.9, ...), custom_call_target="tpu_custom_call" | custom-call | tf_op jit(solution)/shard_map/mgrit/pallas_call | solution.py:461
  68.6 0.0 copy-start
  68.6 1.6 %copy.14 = f32[1,64,512]{2,1,0:T(8,128)} copy(f32[1,64,512]{2,1,0:T(8,128)} %get-tuple-element.4) | data formatting | bytes 262144
  70.2 0.0 copy-done
  70.2 0.7 copy.15
Async XLA Ops:
  0.6 0.7 copy-start.1
  68.6 1.6 %copy-start = (f32[1,64,512]{2,1,0:T(8,128)S(1)}, f32[1,64,512]{2,1,0:T(8,128)}, u32[]{:S(2)}) copy-start(f32[1,64,512]{2,1,0:T(8,128)} %get-tuple-element.5) | copy-start | bytes 393220

commit v2 on v1

--- a/solution.py
+++ b/solution.py
@@ -41,6 +41,7 @@
     c_ref, f_ref,
     gb, ib, gr, br, hs, hr, st, hsrc, hand, cs, cr,
     ohl, ohn, oh4, oh5, oh4t, oh5t, rm, pm, mi, ms, xs, ws, bs, zs, ps, scale, near,
+    slots_out, slots_in, so_sem, si_sem,
     gs_sem, gr_sem, ps_sem, is_sem, br_sem, hs_sem, hr_sem, ts_sem, tr_sem, cs_sem, cr_sem,
 ):
     k = lax.axis_index("tm")
@@ -87,14 +88,15 @@
     def bucketed(value):
         return dot(send_mat, jnp.concatenate(split(value), axis=0)).reshape(n_sp, bk, CELLS)
 
-    slot_tile = jnp.broadcast_to(slot_col, (rows, 128)).reshape(n_sp, bk, 128)
-    gb[:, :, :CELLS] = bucketed(guess_ref[0])
-    gb[:, :, CELLS:] = slot_tile
+    spot = iota((n_sp, bk, 128), 1) == iota((n_sp, bk, 128), 2)
+    slot_wide = jnp.broadcast_to(slot_col, (rows, 128)).reshape(n_sp, bk, 128)
+    slot_lanes = jnp.sum(jnp.where(spot, slot_wide, 0.0), axis=1, keepdims=True)
+    slots_out[...] = jnp.broadcast_to(slot_lanes, (n_sp, 8, 128))
+    gb[...] = bucketed(guess_ref[0])
 
     @pl.when(k == 0)
     def _():
-        ib[:, :, :CELLS] = bucketed(init_ref[...])
-        ib[:, :, CELLS:] = slot_tile
+        ib[...] = bucketed(init_ref[...])
 
     sides = jnp.minimum(k, 1) + jnp.minimum(n_tm - 1 - k, 1)
     pl.semaphore_wait(barrier, (n_sp - 1) * (1 + sides) + n_tm - 1)
@@ -108,7 +110,7 @@
     def own_copy(off):
         to = lax.rem(s + off, n_sp)
         return pltpu.make_async_remote_copy(
-            src_ref=gb.at[to, :, pl.ds(0, CELLS)], dst_ref=gr.at[s], send_sem=gs_sem.at[off],
+            src_ref=gb.at[to], dst_ref=gr.at[s], send_sem=gs_sem.at[off],
             recv_sem=gr_sem.at[s], device_id=(k, to), device_id_type=MESH)
 
     def spread_landed(off):
@@ -121,9 +123,25 @@
     def own_landed(off):
         origin = lax.rem(s + off, n_sp)
         pltpu.make_async_remote_copy(
-            src_ref=gb.at[origin, :, pl.ds(0, CELLS)], dst_ref=gr.at[origin],
+            src_ref=gb.at[origin], dst_ref=gr.at[origin],
             send_sem=gs_sem.at[off], recv_sem=gr_sem.at[origin], device_id=(k, origin),
             device_id_type=MESH).wait_recv()
+
+    def slots_copy(off):
+        to = lax.rem(s + off, n_sp)
+        return pltpu.make_async_remote_copy(
+            src_ref=slots_out.at[to], dst_ref=slots_in.at[s], send_sem=so_sem.at[off],
+            recv_sem=si_sem.at[s], device_id=(k, to), device_id_type=MESH)
+
+    def slots_landed(off):
+        origin = lax.rem(s + off, n_sp)
+        pltpu.make_async_remote_copy(
+            src_ref=slots_out.at[origin], dst_ref=slots_in.at[origin], send_sem=so_sem.at[off],
+            recv_sem=si_sem.at[origin], device_id=(k, origin), device_id_type=MESH).wait_recv()
+
+    for off in range(1, n_sp):
+        slots_copy(off).start()
+    slots_in[s] = slots_out[s]
 
     @pl.when(k == 0)
     def _():
@@ -180,9 +198,7 @@
             halo_down(slot).wait_recv()
 
     exchange(setup)
-    for off in range(1, n_sp):
-        own_copy(off).start()
-    gr[s] = gb[s, :, :CELLS]
+    gr[s] = gb[s]
 
     lane_nb = iota((nb, nb), 1)
     for face in range(6):
@@ -300,6 +316,12 @@
             hs[slot, 0] = top
             hs[slot, 1] = bottom
             exchange(slot)
+            for off in range(1, n_sp):
+                turn = (off - 1) * 4 // (n_sp - 1)
+
+                @pl.when((k == n_tm - 1) & (slot == turn))
+                def _():
+                    own_copy(off).start()
             sums = inside(tiles)
             up_cross = gathered(oh4t[...], bottom)
             down_cross = gathered(oh5t[...], top)
@@ -336,20 +358,33 @@
     def _():
         spread_landed(0)
 
-    arrived = br[...].reshape(rows, CELLS + 128)
-    slots = arrived[:, CELLS:CELLS + nb]
+    for off in range(1, n_sp):
+        slots_landed(off)
+    slots = jnp.sum(jnp.where(spot, slots_in[:, :1], 0.0), axis=2, keepdims=True)
+    slots = jnp.broadcast_to(slots, (n_sp, bk, nb)).reshape(rows, nb)
     take = jnp.where(slots == iota((rows, nb), 1).astype(F32), 1.0, 0.0).T.astype(BF16)
 
     def settled(value):
         high, low = split(value)
         return dot(take, high) + dot(take, low)
 
-    bs[...] = settled(arrived[:, :CELLS])
+    bs[...] = settled(br[...].reshape(rows, CELLS))
 
     def hand_copy(it):
         return pltpu.make_async_remote_copy(
             src_ref=hsrc.at[it], dst_ref=hand.at[it], send_sem=ts_sem.at[it], recv_sem=tr_sem.at[it],
             device_id=(lax.rem(k + 1, n_tm), s), device_id_type=MESH)
+
+    def back_copy():
+        return pltpu.make_async_remote_copy(
+            src_ref=hsrc.at[ITERS - 1], dst_ref=st.at[0], send_sem=ts_sem.at[ITERS - 1],
+            recv_sem=tr_sem.at[ITERS - 1], device_id=(lax.rem(k + n_tm - 1, n_tm), s),
+            device_id_type=MESH)
+
+    @pl.when(k > 0)
+    def _():
+        hsrc[ITERS - 1] = bs[...]
+        back_copy().start()
 
     def coarse_copy(it, off):
         return pltpu.make_async_remote_copy(
@@ -376,7 +411,11 @@
 
         lax.fori_loop(0, 2, one, 0)
 
-        @pl.when(it == 0)
+        @pl.when((it == 0) & (k < n_tm - 1))
+        def _():
+            back_copy().wait_recv()
+
+        @pl.when((it == 0) & (k == n_tm - 1))
         def _():
             for off in range(1, n_sp):
                 own_landed(off)
@@ -415,7 +454,16 @@
     c_ref[0] = st[ITERS]
 
     for off in range(1, n_sp):
-        own_copy(off).wait_send()
+        slots_copy(off).wait_send()
+
+    @pl.when(k == n_tm - 1)
+    def _():
+        for off in range(1, n_sp):
+            own_copy(off).wait_send()
+
+    @pl.when(k > 0)
+    def _():
+        back_copy().wait_send()
 
     @pl.when(k == 0)
     def _():
@@ -465,10 +513,10 @@
             in_specs=[pl.BlockSpec(memory_space=pltpu.VMEM)] * 9,
             out_specs=[pl.BlockSpec(memory_space=pltpu.VMEM)] * 2,
             scratch_shapes=[
-                pltpu.VMEM((n_sp, bk, CELLS + 128), F32),
-                pltpu.VMEM((n_sp, bk, CELLS + 128), F32),
                 pltpu.VMEM((n_sp, bk, CELLS), F32),
-                pltpu.VMEM((n_sp, bk, CELLS + 128), F32),
+                pltpu.VMEM((n_sp, bk, CELLS), F32),
+                pltpu.VMEM((n_sp, bk, CELLS), F32),
+                pltpu.VMEM((n_sp, bk, CELLS), F32),
                 pltpu.VMEM((slots, 2, nb, 128), F32),
                 pltpu.VMEM((slots, 2, nb, 128), F32),
                 pltpu.VMEM((ITERS + 1, nb, CELLS), F32),
@@ -493,6 +541,9 @@
                 pltpu.VMEM((nb, 128), F32),
                 pltpu.VMEM((3, nb, 128), F32),
                 pltpu.VMEM((2, nb, 128), F32),
+                pltpu.VMEM((n_sp, 8, 128), F32),
+                pltpu.VMEM((n_sp, 8, 128), F32),
+                dma((n_sp,)), dma((n_sp,)),
                 dma((n_sp,)), dma((n_sp,)), dma((n_sp,)), dma((n_sp,)), dma((n_sp,)),
                 dma((slots, 2)), dma((slots, 2)),
                 dma((ITERS,)), dma((ITERS,)),

time: 71.9 us -> 66.7 us (0.928)
  Pallas kernels: 66.6 us -> 61.6 us
    pallas_call x1, Pallas kernels: 66.6 us -> 61.6 us  [body(): pl.pallas_call(functools.partial(kernel, n_tm, n_sp, bk), name='mgrit', o...]
where the time goes in v2:
time: 66.7 us; the launch traced here: 65.9 us
  Pallas kernels  61.6 us (92%)
  local copies, waits for them, and re-layouts  3.65 us (5%)
    pallas_call x1, Pallas kernels, body(): pl.pallas_call(functools.partial(kernel, n_tm, n_sp, bk), name='mgrit', o...  61.6 us
    unnamed x7, local copies, waits for them, and re-layouts  3.65 us

profile of v2, /device:TPU:14, one launch (start us, length us, event | category | flops | bytes accessed | tf_op | source)
XLA Modules:
  0.0 65.9 jit_solution(9225438059011056073)
XLA Ops:
  0.6 0.0 copy-start.1
  0.6 0.7 %copy-done.1 = s32[64,6]{0,1:T(8,128)S(1)} copy-done((s32[64,6]{0,1:T(8,128)S(1)}, s32[64,6]{0,1:T(8,128)}, u32[]{:S(2)}) %copy-start.1) | copy-done | bytes 1560
  1.3 0.7 %copy.11.nb_ref = s32[64,6]{1,0:T(8,128)} copy(s32[64,6]{0,1:T(8,128)S(1)} %copy-done.1) | data formatting | bytes 3072 | tf_op args[4]
  2.0 61.6 %mgrit.1 = (f32[1,64,512]{2,1,0:T(8,128)}, f32[1,64,512]{2,1,0:T(8,128)}) custom-call(f32[64,512]{1,0:T(8,128)} %init_ref.1, f32[1,64,512]{2,1,0:T(8,128)} %guess_ref.1, f32[1,2,64,512]{3,2,1,0:T(8,128)} %source_ref.1, s32[1,64]{1,0:T(1,128)} %bitcast.7, s32[64,6]{1,0:T(8,128)} %copy.11.nb_ref, s32[1,64]{1,0:T(1,128)} %bitcast.8, f32[1,4]{1,0:T(1,128)} %bitcast.9, ...), custom_call_target="tpu_custom_call" | custom-call | tf_op jit(solution)/shard_map/mgrit/pallas_call | solution.py:509
  63.6 0.0 copy-start
  63.6 1.6 %copy.14 = f32[1,64,512]{2,1,0:T(8,128)} copy(f32[1,64,512]{2,1,0:T(8,128)} %get-tuple-element.4) | data formatting | bytes 262144
  65.2 0.0 copy-done
  65.2 0.7 copy.15
Async XLA Ops:
  0.6 0.7 %copy-start.1 = (s32[64,6]{0,1:T(8,128)S(1)}, s32[64,6]{0,1:T(8,128)}, u32[]{:S(2)}) copy-start(s32[64,6]{0,1:T(8,128)} %param.13) | copy-start | bytes 4612
  63.6 1.6 %copy-start = (f32[1,64,512]{2,1,0:T(8,128)S(1)}, f32[1,64,512]{2,1,0:T(8,128)}, u32[]{:S(2)}) copy-start(f32[1,64,512]{2,1,0:T(8,128)} %get-tuple-element.5) | copy-start | bytes 393220

commit v3 on v2

--- a/solution.py
+++ b/solution.py
@@ -163,9 +163,10 @@
     scale[1] = DAMP / (1.0 + 6.0 * dif)
     scale[2] = (1.0 + 6.0 * dif) / DAMP
     lane = iota((nb, 128), 1)
+    linked = [column(nb_ref[face:face + 1, :].astype(F32)).astype(jnp.int32) for face in range(6)]
     table = jnp.where(lane == 4, dif, -1.0)
     for face in range(4):
-        table = jnp.where(lane == face, (nb_ref[:, face:face + 1] - s * nb).astype(F32), table)
+        table = jnp.where(lane == face, (linked[face] - s * nb).astype(F32), table)
     hs[setup, 0] = table
     hs[setup, 1] = table
 
@@ -203,7 +204,7 @@
     lane_nb = iota((nb, nb), 1)
     for face in range(6):
         shift = s * nb + (0 if face < 4 else (-nb if face == 4 else nb))
-        ids = nb_ref[:, face:face + 1]
+        ids = linked[face]
         hot = jnp.where((ids - shift == lane_nb) & (ids >= 0), 1.0, 0.0)
         if face >= 4:
             turned = hot.T
@@ -551,7 +552,7 @@
             ],
             compiler_params=pltpu.CompilerParams(collective_id=0, has_side_effects=True),
         )(
-            init_state, guess, source, remap.reshape(1, nb), neighbors, block_class.reshape(1, nb),
+            init_state, guess, source, remap.reshape(1, nb), neighbors.T, block_class.reshape(1, nb),
             step_number.reshape(1, CLASSES), inverse.reshape(CLASSES * COARSE, COARSE),
             cstep.reshape(CLASSES * COARSE, COARSE),
         )

time: 66.7 us -> 65.3 us (0.979)
  local copies, waits for them, and re-layouts: 3.65 us -> 2.26 us
    unnamed x7 -> x4, local copies, waits for them, and re-layouts: 3.65 us -> 2.26 us
where the time goes in v3:
time: 65.3 us; the launch traced here: 64.5 us
  Pallas kernels  61.6 us (94%)
  local copies, waits for them, and re-layouts  2.26 us (3%)
    pallas_call x1, Pallas kernels, body(): pl.pallas_call(functools.partial(kernel, n_tm, n_sp, bk), name='mgrit', o...  61.6 us
    unnamed x4, local copies, waits for them, and re-layouts  2.26 us

profile of v3, /device:TPU:14, one launch (start us, length us, event | category | flops | bytes accessed | tf_op | source)
XLA Modules:
  0.0 64.5 jit_solution(14414524264015680802)
XLA Ops:
  0.6 61.6 %mgrit.1 = (f32[1,64,512]{2,1,0:T(8,128)}, f32[1,64,512]{2,1,0:T(8,128)}) custom-call(f32[64,512]{1,0:T(8,128)} %init_ref.1, f32[1,64,512]{2,1,0:T(8,128)} %guess_ref.1, f32[1,2,64,512]{3,2,1,0:T(8,128)} %source_ref.1, s32[1,64]{1,0:T(1,128)} %bitcast.9, s32[6,64]{1,0:T(8,128)} %bitcast.8, s32[1,64]{1,0:T(1,128)} %bitcast.10, f32[1,4]{1,0:T(1,128)} %bitcast.11, ...), custom_call_target="tpu_custom_call" | custom-call | tf_op jit(solution)/shard_map/mgrit/pallas_call | solution.py:510
  62.2 0.0 copy-start
  62.2 1.6 %copy.13 = f32[1,64,512]{2,1,0:T(8,128)} copy(f32[1,64,512]{2,1,0:T(8,128)} %get-tuple-element.4) | data formatting | bytes 262144
  63.8 0.0 copy-done
  63.8 0.7 %copy.14 = f32[1,64,512]{2,1,0:T(8,128)} copy(f32[1,64,512]{2,1,0:T(8,128)S(1)} %copy-done) | data formatting | bytes 262144
Async XLA Ops:
  62.2 1.6 %copy-start = (f32[1,64,512]{2,1,0:T(8,128)S(1)}, f32[1,64,512]{2,1,0:T(8,128)}, u32[]{:S(2)}) copy-start(f32[1,64,512]{2,1,0:T(8,128)} %get-tuple-element.5) | copy-start | bytes 393220
